TPU v7x, 256 devices: a whole 4x4x8 slice. The times are simulated.
256 devices in a mesh: dp: 4 (over x), row: 8 (over z_lo, core), col: 8 (over z_hi, y).
Axes of the slice: x: 4, y: 4, z: 8 (z_hi: 2, z_lo: 4; z = z_hi * 4 + z_lo), core: 2. Of those that a mesh axis runs over, the one named last changes fastest.
Arguments:
- tokens: bfloat16 [4096, 8192], P(('dp', 'col'), 'row'), may hold values from -6 to 6
- gate_weight: bfloat16 [8192, 14336], P('row', ('dp', 'col')), may hold values from -0.0625 to 0.0625
- up_weight: bfloat16 [8192, 14336], P('row', ('dp', 'col')), may hold values from -0.0625 to 0.0625
- down_weight: bfloat16 [14336, 8192], P(('dp', 'col'), 'row'), may hold values from -0.046875 to 0.046875
Outputs:
- mixed: bfloat16 [4096, 8192], P(('dp', 'col'), 'row')
All inputs are finite; a program needn't handle non-finite values.
Results may differ from a plain program's by a relative error of at most 0.03.
Values may be sent and summed in bfloat16 or wider, within the bound.
A program may use at most 64 MiB of HBM per device.

v0:
```python
import jax
import jax.numpy as jnp
from jax import lax
from jax.sharding import PartitionSpec as P


def on_device(tokens, gate_weight, up_weight, down_weight):
    group_tokens = lax.all_gather(tokens, "col", axis=0, tiled=True)
    gate_cols, up_cols = (
        lax.all_gather(gate_weight, "dp", axis=1, tiled=True),
        lax.all_gather(up_weight, "dp", axis=1, tiled=True),
    )
    gate_term = jnp.dot(group_tokens, gate_cols, preferred_element_type=jnp.float32)
    up_term = jnp.dot(group_tokens, up_cols, preferred_element_type=jnp.float32)
    row_sums = lax.psum_scatter(
        jnp.concatenate((gate_term, up_term), axis=1).astype(jnp.bfloat16),
        "row",
        scatter_dimension=0,
        tiled=True,
    ).astype(jnp.float32)
    half_width = gate_cols.shape[1]
    gate_sum = row_sums[:, :half_width]
    up_sum = row_sums[:, half_width:]
    hidden = (jax.nn.silu(gate_sum) * up_sum).astype(jnp.bfloat16)
    hidden_all = lax.all_gather(hidden, "row", axis=0, tiled=True)
    down_term = jnp.dot(
        hidden_all,
        lax.all_gather(down_weight, "dp", axis=0, tiled=True),
        preferred_element_type=jnp.float32,
    )
    mixed = lax.psum_scatter(down_term.astype(jnp.bfloat16), "col", scatter_dimension=0, tiled=True)
    return mixed


def solution(mesh):
    return jax.shard_map(
        on_device,
        mesh=mesh,
        in_specs=(
            P(("dp", "col"), "row"),
            P("row", ("dp", "col")),
            P("row", ("dp", "col")),
            P(("dp", "col"), "row"),
        ),
        out_specs=P(("dp", "col"), "row"),
        check_vma=False,
    )
```

profile of v0, /device:TPU:2, one launch (start us, length us, event | category | flops | bytes accessed | tf_op | source)
XLA Modules:
  0.0 489.1 jit_solution(3508342044773073556)
XLA Ops:
  6.5 0.7 all-gather.6.cloned.1.call-update
  7.3 0.0 all-gather.8.cloned.1.call-start
  7.3 0.7 all-gather.8.cloned.1.call-update
  8.0 0.0 all-gather.10.cloned.1.call-start
  8.1 0.7 all-gather.10.cloned.1.call-update
  8.7 0.0 reduce-scatter.3.cloned.1.call-start
  8.8 80.1 %all-gather.6.cloned.1.call-done = bf16[1024,1024]{1,0:T(8,128)(2,1)} async-done(((bf16[128,1024]{1,0:T(8,128)(2,1)}), bf16[1024,1024]{1,0:T(8,128)(2,1)}) %all-gather.6.cloned.1.call-update) | async-done | bytes 2097168 | tf_op jit(solution)/shard_map/all_gather | solution.py:8
  88.9 43.2 %all-gather.8.cloned.1.call-done = bf16[1024,1792]{0,1:T(8,128)(2,1)} async-done(((bf16[1024,448]{0,1:T(8,128)(2,1)}), bf16[1024,1792]{0,1:T(8,128)(2,1)}) %all-gather.8.cloned.1.call-update) | async-done | bytes 3670032 | tf_op jit(solution)/shard_map/all_gather | solution.py:10
  132.1 8.5 %convolution_convert_fusion.1 = bf16[1024,1792]{1,0:T(8,128)(2,1)} fusion(bf16[1024,1024]{1,0:T(8,128)(2,1)} %all-gather.6.cloned.1.call-done, bf16[1024,1792]{0,1:T(8,128)(2,1)} %all-gather.8.cloned.1.call-done), kind=kOutput, calls=%fused_computation.2 | convolution fusion | flops 3759931392 | bytes 9437184 | tf_op jit(solution)/shard_map/dot_general | solution.py:13
  140.6 40.0 %all-gather.10.cloned.1.call-done = bf16[1024,1792]{0,1:T(8,128)(2,1)} async-done(((bf16[1024,448]{0,1:T(8,128)(2,1)}), bf16[1024,1792]{0,1:T(8,128)(2,1)}) %all-gather.10.cloned.1.call-update) | async-done | bytes 3670032 | tf_op jit(solution)/shard_map/all_gather | solution.py:11
  180.6 8.7 %convolution_convert_fusion = bf16[1024,1792]{1,0:T(8,128)(2,1)} fusion(bf16[1024,1024]{1,0:T(8,128)(2,1)} %all-gather.6.cloned.1.call-done, bf16[1024,1792]{0,1:T(8,128)(2,1)} %all-gather.10.cloned.1.call-done), kind=kOutput, calls=%fused_computation.1 | convolution fusion | flops 3759931392 | bytes 9437184 | tf_op jit(solution)/shard_map/dot_general | solution.py:14
  189.3 5.5 %pad_maximum_fusion = bf16[1024,3584]{1,0:T(8,128)(2,1)} fusion(bf16[1024,1792]{1,0:T(8,128)(2,1)} %convolution_convert_fusion, bf16[1024,1792]{1,0:T(8,128)(2,1)S(1)} %copy-done), kind=kLoop, calls=%fused_computation | loop fusion | flops 14680064 | bytes 14680064 | tf_op jit(solution)/shard_map/concatenate | solution.py:16
  194.8 0.0 reduce-scatter.3.cloned.1.call-update
  194.9 0.0 all-gather.14.cloned.1.call-start
  194.9 0.5 all-gather.14.cloned.1.call-update
  195.5 0.0 all-gather.12.cloned.1.call-start
  195.5 85.4 %reduce-scatter.3.cloned.1.call-done = bf16[128,3584]{1,0:T(8,128)(2,1)} async-done(((bf16[1024,3584]{1,0:T(8,128)(2,1)}), bf16[128,3584]{1,0:T(8,128)(2,1)}) %reduce-scatter.3.cloned.1.call-update) | async-done | bytes 917520 | tf_op jit(solution)/shard_map/reduce_scatter | solution.py:15
  280.9 1.4 convert_element_type.10
  282.3 1.0 fusion
  283.3 0.0 reduce-scatter.5.cloned.1.call-start
  283.4 43.5 %all-gather.14.cloned.1.call-done = bf16[1792,1024]{1,0:T(8,128)(2,1)} async-done(((bf16[448,1024]{1,0:T(8,128)(2,1)}), bf16[1792,1024]{1,0:T(8,128)(2,1)}) %all-gather.14.cloned.1.call-update) | async-done | bytes 3670032 | tf_op jit(solution)/shard_map/all_gather | solution.py:28
  326.9 52.3 %all-gather.12.cloned.1.call-done = bf16[1024,1792]{1,0:T(8,128)(2,1)} async-done(((bf16[128,1792]{1,0:T(8,128)(2,1)}), bf16[1024,1792]{1,0:T(8,128)(2,1)}) %all-gather.12.cloned.1.call-update) | async-done | bytes 3670032 | tf_op jit(solution)/shard_map/all_gather | solution.py:25
  379.2 8.4 %convolution_convert_fusion.2 = bf16[1024,1024]{1,0:T(8,128)(2,1)} fusion(bf16[1024,1792]{1,0:T(8,128)(2,1)} %all-gather.12.cloned.1.call-done, bf16[1792,1024]{1,0:T(8,128)(2,1)} %all-gather.14.cloned.1.call-done), kind=kOutput, calls=%fused_computation.3 | convolution fusion | flops 3759144960 | bytes 9437184 | tf_op jit(solution)/shard_map/dot_general | solution.py:26
  387.6 94.6 %reduce-scatter.5.cloned.1.call-done = bf16[128,1024]{1,0:T(8,128)(2,1)} async-done(((bf16[1024,1024]{1,0:T(8,128)(2,1)}), bf16[128,1024]{1,0:T(8,128)(2,1)}) %reduce-scatter.5.cloned.1.call-update) | async-done | bytes 262160 | tf_op jit(solution)/shard_map/reduce_scatter | solution.py:31
  (5 shorter events, 0.0 us)
Async XLA Ops:
  6.5 82.4 %all-gather.6.cloned.1.call-start = ((), (), s32[]{:S(2)}) async-start(), calls=%async_computation.2 | async-start | bytes 2359296 | tf_op jit(solution)/shard_map/all_gather | solution.py:8
  7.3 124.9 %all-gather.8.cloned.1.call-start = ((), (), s32[]{:S(2)}) async-start(), calls=%async_computation.3 | async-start | bytes 4587520 | tf_op jit(solution)/shard_map/all_gather | solution.py:10
  8.0 172.6 %all-gather.10.cloned.1.call-start = ((), (), s32[]{:S(2)}) async-start(), calls=%async_computation.4 | async-start | bytes 4587520 | tf_op jit(solution)/shard_map/all_gather | solution.py:11
  8.7 272.2 %reduce-scatter.3.cloned.1.call-start = ((), (), s32[]{:S(2)}) async-start(), calls=%async_computation.5 | async-start | bytes 8257536 | tf_op jit(solution)/shard_map/reduce_scatter | solution.py:15
  180.6 8.7 %copy-start = (bf16[1024,1792]{1,0:T(8,128)(2,1)S(1)}, bf16[1024,1792]{1,0:T(8,128)(2,1)}, u32[]{:S(2)}) copy-start(bf16[1024,1792]{1,0:T(8,128)(2,1)} %convolution_convert_fusion.1) | copy-start | bytes 11010052
  194.9 132.0 %all-gather.14.cloned.1.call-start = ((), (), s32[]{:S(2)}) async-start(), calls=%async_computation.7 | async-start | bytes 4587520 | tf_op jit(solution)/shard_map/all_gather | solution.py:28
  195.5 183.7 %all-gather.12.cloned.1.call-start = ((), (), s32[]{:S(2)}) async-start(), calls=%async_computation.6 | async-start | bytes 4128768 | tf_op jit(solution)/shard_map/all_gather | solution.py:25
  283.3 198.9 %reduce-scatter.5.cloned.1.call-start = ((), (), s32[]{:S(2)}) async-start(), calls=%async_computation.8 | async-start | bytes 2359296 | tf_op jit(solution)/shard_map/reduce_scatter | solution.py:31
Sparse Core Ops, SparseCore 0:
  10.0 78.8 all-gather.5
  90.7 41.3 all-gather.7
  133.9 46.6 all-gather.9
  195.0 85.8 reduce-scatter.2
  282.6 44.2 all-gather.13
  328.5 50.5 all-gather.11
  387.7 94.4 reduce-scatter.4
where the time goes:
time: 489 us
  waiting for transfers between devices  442 us (90%)
  matrix products  25.7 us (5%)
  between operations  13.5 us (3%)
  other arithmetic  7.89 us (2%)
    reduce_scatter x1, waiting for transfers between devices, on_device(): lax.psum_scatter(down_term.astype(jnp.bfloat16), 'col', scatter_dimension...  94.6 us
    reduce_scatter x1, waiting for transfers between devices, on_device(): lax.psum_scatter(jnp.concatenate((gate_term, up_term), axis=1).astype(jnp...  85.4 us
    all_gather x1, waiting for transfers between devices, on_device(): group_tokens = lax.all_gather(tokens, 'col', axis=0, tiled=True)  80.1 us
    all_gather x1, waiting for transfers between devices, on_device(): hidden_all = lax.all_gather(hidden, 'row', axis=0, tiled=True)  52.3 us
    all_gather x1, waiting for transfers between devices, on_device(): lax.all_gather(down_weight, 'dp', axis=0, tiled=True)  43.5 us
    all_gather x1, waiting for transfers between devices, on_device(): lax.all_gather(gate_weight, 'dp', axis=1, tiled=True)  43.2 us
    all_gather x1, waiting for transfers between devices, on_device(): lax.all_gather(up_weight, 'dp', axis=1, tiled=True)  40 us
  transfers between devices with their start and end apart: 7, of which 7 were waited for; matrix products, arithmetic and copies ran while one was open for 2% of the time, Pallas kernels for 0%

commit v1 on v0

--- a/solution.py
+++ b/solution.py
@@ -7,7 +7,9 @@
 def on_device(tokens, gate_weight, up_weight, down_weight):
     group_tokens = lax.all_gather(tokens, "col", axis=0, tiled=True)
     gate_cols, up_cols = (
-        lax.all_gather(gate_weight, "dp", axis=1, tiled=True),
+        jnp.concatenate(
+            lax.all_to_all(jnp.stack([gate_weight] * lax.axis_size("dp")), "dp", 0, 0), axis=1
+        ),
         lax.all_gather(up_weight, "dp", axis=1, tiled=True),
     )
     gate_term = jnp.dot(group_tokens, gate_cols, preferred_element_type=jnp.float32)

time: 489 us -> 441 us (0.902)
  waiting for transfers between devices: 442 us -> 345 us
  blocking collectives: 0 us -> 46.5 us
    all_gather x1, waiting for transfers between devices: 80.1 us -> 32.7 us  [on_device(): group_tokens = lax.all_gather(tokens, 'col', axis=0, tiled=True)]
    all_to_all x0 -> x1, blocking collectives: none -> 46.5 us  [on_device(): lax.all_to_all(jnp.stack([gate_weight] * lax.axis_size('dp')), 'dp', 0, 0)]
    all_gather x1 -> x0, waiting for transfers between devices: 43.2 us -> none  [on_device(): lax.all_gather(gate_weight, 'dp', axis=1, tiled=True)]
    all_gather x1, waiting for transfers between devices: 40 us -> 34.7 us  [on_device(): lax.all_gather(up_weight, 'dp', axis=1, tiled=True)]
  transfers between devices with their start and end apart: 7 -> 6, of which waited for: 7 -> 6; matrix products, arithmetic and copies ran while one was open for 2% -> 3% of each run, Pallas kernels for 0% -> 0%
where the time goes in v1:
time: 441 us
  waiting for transfers between devices  345 us (78%)
  blocking collectives  46.5 us (11%)
  matrix products  25.7 us (6%)
  between operations  13.5 us (3%)
  other arithmetic  7.88 us (2%)
    reduce_scatter x1, waiting for transfers between devices, on_device(): lax.psum_scatter(down_term.astype(jnp.bfloat16), 'col', scatter_dimension...  94.7 us
    reduce_scatter x1, waiting for transfers between devices, on_device(): lax.psum_scatter(jnp.concatenate((gate_term, up_term), axis=1).astype(jnp...  85.4 us
    all_gather x1, waiting for transfers between devices, on_device(): hidden_all = lax.all_gather(hidden, 'row', axis=0, tiled=True)  52.3 us
    all_to_all x1, blocking collectives, on_device(): lax.all_to_all(jnp.stack([gate_weight] * lax.axis_size('dp')), 'dp', 0, 0)  46.5 us
    all_gather x1, waiting for transfers between devices, on_device(): lax.all_gather(down_weight, 'dp', axis=0, tiled=True)  43.5 us
    all_gather x1, waiting for transfers between devices, on_device(): lax.all_gather(up_weight, 'dp', axis=1, tiled=True)  34.7 us
    all_gather x1, waiting for transfers between devices, on_device(): group_tokens = lax.all_gather(tokens, 'col', axis=0, tiled=True)  32.7 us
  transfers between devices with their start and end apart: 6, of which 6 were waited for; matrix products, arithmetic and copies ran while one was open for 3% of the time, Pallas kernels for 0%

profile of v1, /device:TPU:2, one launch (start us, length us, event | category | flops | bytes accessed | tf_op | source)
XLA Modules:
  0.0 440.6 jit_solution(13592587640558273527)
XLA Ops:
  6.5 0.7 all-gather.5.cloned.1.call-update
  7.3 0.0 all-gather.7.cloned.1.call-start
  7.3 0.7 all-gather.7.cloned.1.call-update
  8.0 0.0 reduce-scatter.3.cloned.1.call-start
  8.1 1.6 stack.2
  9.7 46.5 %all_to_all.5 = bf16[4,1024,448]{1,2,0:T(8,128)(2,1)} all-to-all(bf16[4,1024,448]{1,2,0:T(8,128)(2,1)S(1)} %stack.2), channel_id=1, replica_groups=mesh['dp'=4,'row'=8,'col'=8] {'dp'}, dimensions={0} | all-to-all | bytes 7340032 | tf_op jit(solution)/shard_map/all_to_all | solution.py:11
  56.2 32.7 %all-gather.5.cloned.1.call-done = bf16[1024,1024]{1,0:T(8,128)(2,1)} async-done(((bf16[128,1024]{1,0:T(8,128)(2,1)}), bf16[1024,1024]{1,0:T(8,128)(2,1)}) %all-gather.5.cloned.1.call-update) | async-done | bytes 2097168 | tf_op jit(solution)/shard_map/all_gather | solution.py:8
  88.9 8.5 %convolution_convert_fusion.1 = bf16[1024,1792]{1,0:T(8,128)(2,1)} fusion(bf16[1024,1024]{1,0:T(8,128)(2,1)} %all-gather.5.cloned.1.call-done, bf16[1024,1792]{0,1:T(8,128)(2,1)} %bitcast.9), kind=kOutput, calls=%fused_computation.2 | convolution fusion | flops 3759931392 | bytes 9437184 | tf_op jit(solution)/shard_map/dot_general | solution.py:15
  97.4 34.7 %all-gather.7.cloned.1.call-done = bf16[1024,1792]{0,1:T(8,128)(2,1)} async-done(((bf16[1024,448]{0,1:T(8,128)(2,1)}), bf16[1024,1792]{0,1:T(8,128)(2,1)}) %all-gather.7.cloned.1.call-update) | async-done | bytes 3670032 | tf_op jit(solution)/shard_map/all_gather | solution.py:13
  132.1 8.7 %convolution_convert_fusion = bf16[1024,1792]{1,0:T(8,128)(2,1)} fusion(bf16[1024,1024]{1,0:T(8,128)(2,1)} %all-gather.5.cloned.1.call-done, bf16[1024,1792]{0,1:T(8,128)(2,1)} %all-gather.7.cloned.1.call-done), kind=kOutput, calls=%fused_computation.1 | convolution fusion | flops 3759931392 | bytes 9437184 | tf_op jit(solution)/shard_map/dot_general | solution.py:16
  140.8 5.5 %pad_maximum_fusion = bf16[1024,3584]{1,0:T(8,128)(2,1)} fusion(bf16[1024,1792]{1,0:T(8,128)(2,1)} %convolution_convert_fusion, bf16[1024,1792]{1,0:T(8,128)(2,1)S(1)} %copy-done), kind=kLoop, calls=%fused_computation | loop fusion | flops 14680064 | bytes 14680064 | tf_op jit(solution)/shard_map/concatenate | solution.py:18
  146.3 0.0 reduce-scatter.3.cloned.1.call-update
  146.4 0.0 all-gather.11.cloned.1.call-start
  146.4 0.5 all-gather.11.cloned.1.call-update
  146.9 0.0 all-gather.9.cloned.1.call-start
  147.0 85.4 %reduce-scatter.3.cloned.1.call-done = bf16[128,3584]{1,0:T(8,128)(2,1)} async-done(((bf16[1024,3584]{1,0:T(8,128)(2,1)}), bf16[128,3584]{1,0:T(8,128)(2,1)}) %reduce-scatter.3.cloned.1.call-update) | async-done | bytes 917520 | tf_op jit(solution)/shard_map/reduce_scatter | solution.py:17
  232.4 1.4 convert_element_type.10
  233.8 1.0 fusion
  234.8 0.0 all-gather.9.cloned.1.call-update
  234.8 0.0 reduce-scatter.5.cloned.1.call-start
  234.9 43.5 %all-gather.11.cloned.1.call-done = bf16[1792,1024]{1,0:T(8,128)(2,1)} async-done(((bf16[448,1024]{1,0:T(8,128)(2,1)}), bf16[1792,1024]{1,0:T(8,128)(2,1)}) %all-gather.11.cloned.1.call-update) | async-done | bytes 3670032 | tf_op jit(solution)/shard_map/all_gather | solution.py:30
  278.4 52.3 %all-gather.9.cloned.1.call-done = bf16[1024,1792]{1,0:T(8,128)(2,1)} async-done(((bf16[128,1792]{1,0:T(8,128)(2,1)}), bf16[1024,1792]{1,0:T(8,128)(2,1)}) %all-gather.9.cloned.1.call-update) | async-done | bytes 3670032 | tf_op jit(solution)/shard_map/all_gather | solution.py:27
  330.6 8.4 %convolution_convert_fusion.2 = bf16[1024,1024]{1,0:T(8,128)(2,1)} fusion(bf16[1024,1792]{1,0:T(8,128)(2,1)} %all-gather.9.cloned.1.call-done, bf16[1792,1024]{1,0:T(8,128)(2,1)} %all-gather.11.cloned.1.call-done), kind=kOutput, calls=%fused_computation.3 | convolution fusion | flops 3759144960 | bytes 9437184 | tf_op jit(solution)/shard_map/dot_general | solution.py:28
  339.1 94.7 %reduce-scatter.5.cloned.1.call-done = bf16[128,1024]{1,0:T(8,128)(2,1)} async-done(((bf16[1024,1024]{1,0:T(8,128)(2,1)}), bf16[128,1024]{1,0:T(8,128)(2,1)}) %reduce-scatter.5.cloned.1.call-update) | async-done | bytes 262160 | tf_op jit(solution)/shard_map/reduce_scatter | solution.py:33
  (4 shorter events, 0.0 us)
Async XLA Ops:
  6.5 82.4 %all-gather.5.cloned.1.call-start = ((), (), s32[]{:S(2)}) async-start(), calls=%async_computation.3 | async-start | bytes 2359296 | tf_op jit(solution)/shard_map/all_gather | solution.py:8
  7.3 124.9 %all-gather.7.cloned.1.call-start = ((), (), s32[]{:S(2)}) async-start(), calls=%async_computation.4 | async-start | bytes 4587520 | tf_op jit(solution)/shard_map/all_gather | solution.py:13
  8.0 224.4 %reduce-scatter.3.cloned.1.call-start = ((), (), s32[]{:S(2)}) async-start(), calls=%async_computation.5 | async-start | bytes 8257536 | tf_op jit(solution)/shard_map/reduce_scatter | solution.py:17
  132.1 8.7 %copy-start = (bf16[1024,1792]{1,0:T(8,128)(2,1)S(1)}, bf16[1024,1792]{1,0:T(8,128)(2,1)}, u32[]{:S(2)}) copy-start(bf16[1024,1792]{1,0:T(8,128)(2,1)} %convolution_convert_fusion.1) | copy-start | bytes 11010052
  146.4 132.0 %all-gather.11.cloned.1.call-start = ((), (), s32[]{:S(2)}) async-start(), calls=%async_computation.7 | async-start | bytes 4587520 | tf_op jit(solution)/shard_map/all_gather | solution.py:30
  146.9 183.7 %all-gather.9.cloned.1.call-start = ((), (), s32[]{:S(2)}) async-start(), calls=%async_computation.6 | async-start | bytes 4128768 | tf_op jit(solution)/shard_map/all_gather | solution.py:27
  234.8 199.0 %reduce-scatter.5.cloned.1.call-start = ((), (), s32[]{:S(2)}) async-start(), calls=%async_computation.8 | async-start | bytes 2359296 | tf_op jit(solution)/shard_map/reduce_scatter | solution.py:33
Sparse Core Ops, SparseCore 0:
  10.0 78.8 all-gather.4
  90.7 41.3 all-gather.6
  146.5 85.8 reduce-scatter.2
  234.1 44.2 all-gather.10
  280.0 50.5 all-gather.8
  339.2 94.5 reduce-scatter.4
